TPU v7x, 256 devices: a whole 4x4x8 slice. The times are simulated.
256 devices in a mesh: fsdp: 32 (over z_hi, y, core), tp: 8 (over z_lo, x).
Axes of the slice: x: 4, y: 4, z: 8 (z_hi: 4, z_lo: 2; z = z_hi * 2 + z_lo), core: 2. Of those that a mesh axis runs over, the one named last changes fastest.
Arguments:
- normed: bfloat16 [32768, 8192], P('fsdp'), may hold values from -6 to 6
- kv_weight: bfloat16 [8192, 2048], P('fsdp', 'tp'), may hold values from -0.0625 to 0.0625
- kv_cotangent: bfloat16 [32768, 2048], P('fsdp', 'tp'), may hold values from -0.25 to 0.25
- first_moment: float32 [8192, 2048], P('fsdp', 'tp'), may hold values from -6 to 6
- second_moment: float32 [8192, 2048], P('fsdp', 'tp'), may hold values from 0.5 to 5
- cauchy_points: int32 [20], replicated, may hold values from 0 to 19, each once
Outputs:
- keys_values: bfloat16 [32768, 2048], P('fsdp', 'tp')
- new_first: float32 [8192, 2048], P('fsdp', 'tp')
- new_second: float32 [8192, 2048], P('fsdp', 'tp')
- parity: float32 [4, 2, 4096, 256], P(None, None, 'fsdp', 'tp')
Inputs may be any that keep to these rules, and one draw needn't show every extreme that they name: `cauchy_points`: each value once; the first 4 entries are the parity points, the other 16 the members' points in rank order.
All inputs are finite; a program needn't handle non-finite values.
Results may differ from a plain program's by a relative error of at most 0.001.
Values may be sent and summed in bfloat16 or wider, within the bound.
A program may use at most 192 MiB of HBM per device.

v0:
```python
import jax
import jax.numpy as jnp
from jax import lax
from jax.sharding import PartitionSpec as P

GROUP = 16
PARITY = 4
beta_first = 0.9
beta_second = 0.95


def from_partner(shard, axis, bit):
    return lax.ppermute(shard, axis, [(i, i ^ 1 << bit) for i in range(lax.axis_size(axis))])


def halve_rows(values, fsdp_index):
    half_rows = values.shape[2] // 2
    upper = fsdp_index // (1 << 0) % 2
    retained = lax.dynamic_slice_in_dim(values, upper * half_rows, half_rows, 2)
    outgoing = lax.dynamic_slice_in_dim(values, (1 - upper) * half_rows, half_rows, 2)
    values = retained + from_partner(outgoing, "fsdp", 0)
    return values


def local(normed, kv_weight, kv_cotangent, first_moment, second_moment, cauchy_points):
    contract = (((0,), (0,)), ((), ()))
    columns = normed
    projected = jnp.dot(
        columns,
        lax.all_gather(kv_weight, "fsdp", axis=0, tiled=True),
        preferred_element_type=jnp.float32,
    )
    keys_values = projected.astype(jnp.bfloat16)
    columns = normed
    gradient = lax.psum_scatter(
        lax.dot_general(columns, kv_cotangent, contract, preferred_element_type=jnp.float32),
        "fsdp",
        scatter_dimension=0,
        tiled=True,
    )
    new_first = beta_first * first_moment + (1.0 - beta_first) * gradient
    new_second = beta_second * second_moment + (1.0 - beta_second) * gradient * gradient
    points = cauchy_points.astype(jnp.float32)
    cauchy = 1.0 / (points[:PARITY, None] - points[None, PARITY:])
    tp_count = lax.axis_size("tp")
    group_rows = GROUP // tp_count
    fsdp_index = lax.axis_index("fsdp")
    payload = jnp.stack([new_first, new_second])
    member_rank = fsdp_index % group_rows * tp_count + lax.axis_index("tp")
    selector = (jnp.arange(GROUP, dtype=jnp.int32) == member_rank).astype(jnp.float32)
    column_weights = jnp.sum(cauchy * selector[None, :], axis=1)
    contribution = column_weights[:, None, None, None] * payload[None]
    summed = lax.psum_scatter(contribution, "tp", scatter_dimension=3, tiled=True)
    parity = halve_rows(summed, fsdp_index)
    return (keys_values, new_first, new_second, parity)


def solution(mesh):
    return jax.shard_map(
        local,
        mesh=mesh,
        in_specs=(
            P("fsdp", None),
            P("fsdp", "tp"),
            P("fsdp", "tp"),
            P("fsdp", "tp"),
            P("fsdp", "tp"),
            P(),
        ),
        out_specs=(P("fsdp", "tp"), P("fsdp", "tp"), P("fsdp", "tp"), P(None, None, "fsdp", "tp")),
        check_vma=False,
    )
```

profile of v0, /device:TPU:1, one launch (start us, length us, event | category | flops | bytes accessed | tf_op | source)
XLA Modules:
  0.0 275.5 jit_solution(3754259046699484786)
XLA Ops:
  7.2 0.0 copy-start
  7.2 0.0 reduce-scatter.3.cloned.1.call-start
  7.2 1.0 copy-done
  8.2 13.7 %fusion.1 = f32[8192,256]{1,0:T(8,128)} fusion(bf16[1024,8192]{1,0:T(8,128)(2,1)} %param.6, bf16[1024,256]{1,0:T(8,128)(2,1)S(1)} %copy-done), kind=kOutput, calls=%fused_computation.10 | convolution fusion | flops 4294967296 | bytes 25690112 | tf_op jit(solution)/shard_map/dot_general | solution.py:36
  22.0 0.0 reduce-scatter.3.cloned.1.call-update
  22.0 0.0 reduce-scatter.5.cloned.1.call-start
  22.0 0.6 copy-done.6
  22.6 0.1 slice.7
  22.7 0.2 multiply_reduce_fusion
  22.9 123.0 %reduce-scatter.3.cloned.1.call-done = f32[256,256]{1,0:T(8,128)} async-done(((f32[8192,256]{1,0:T(8,128)}), f32[256,256]{1,0:T(8,128)}) %reduce-scatter.3.cloned.1.call-update) | async-done | bytes 262160 | tf_op jit(solution)/shard_map/reduce_scatter | solution.py:35
  145.9 1.0 fusion
  146.9 0.0 copy-start.1
  146.9 0.0 copy-start.2
  147.0 0.2 copy.11
  147.2 1.6 broadcast_multiply_fusion
  148.8 0.0 reduce-scatter.5.cloned.1.call-update
  148.8 0.0 all-gather.2.cloned.1.call-start
  148.8 0.7 all-gather.2.cloned.1.call-update
  149.5 39.2 %reduce-scatter.5.cloned.1.call-done = f32[4,2,256,32]{2,3,1,0:T(8,128)} async-done(((f32[4,2,256,256]{2,3,1,0:T(8,128)}), f32[4,2,256,32]{2,3,1,0:T(8,128)}) %reduce-scatter.5.cloned.1.call-update) | async-done | bytes 262160 | tf_op jit(solution)/shard_map/reduce_scatter | solution.py:53
  188.7 0.9 constant_dynamic-slice_fusion
  189.7 5.9 %collective-permute-start = (f32[4,2,128,32]{2,3,1,0:T(8,128)S(1)}, f32[4,2,128,32]{2,3,1,0:T(8,128)S(1)}, u32[]{:S(2)}, u32[]{:S(2)}) collective-permute-start(f32[4,2,128,32]{2,3,1,0:T(8,128)S(1)} %constant_dynamic-slice_fusion), channel_id=1, source_target_pairs={{0,8},{8,0},{16,24},{24,16},{32,40},{40,32},{48,56},{56,48},{64,72... | collective-permute-start | bytes 393224 | tf_op jit(solution)/shard_map/ppermute | solution.py:13
  195.6 60.5 %all-gather.2.cloned.1.call-done = bf16[8192,256]{1,0:T(8,128)(2,1)} async-done(((bf16[256,256]{1,0:T(8,128)(2,1)}), bf16[8192,256]{1,0:T(8,128)(2,1)}) %all-gather.2.cloned.1.call-update) | async-done | bytes 4194320 | tf_op jit(solution)/shard_map/all_gather | solution.py:30
  256.0 12.2 %convolution_convert_fusion = bf16[1024,256]{1,0:T(8,128)(2,1)} fusion(bf16[1024,8192]{1,0:T(8,128)(2,1)} %param.6, bf16[8192,256]{1,0:T(8,128)(2,1)} %all-gather.2.cloned.1.call-done), kind=kOutput, calls=%fused_computation | convolution fusion | flops 4295229440 | bytes 21495808 | tf_op jit(solution)/shard_map/dot_general | solution.py:28
  268.3 0.7 dynamic-slice_add_fusion
  (13 shorter events, 0.1 us)
Async XLA Ops:
  7.2 1.0 copy-start
  7.2 138.7 %reduce-scatter.3.cloned.1.call-start = ((), (), s32[]{:S(2)}) async-start(), calls=%async_computation.3 | async-start | bytes 8650752 | tf_op jit(solution)/shard_map/reduce_scatter | solution.py:35
  22.0 0.7 copy-start.6
  22.0 123.9 %copy-start.3 = (f32[256,256]{1,0:T(8,128)S(1)}, f32[256,256]{1,0:T(8,128)}, u32[]{:S(2)}) copy-start(f32[256,256]{1,0:T(8,128)} %param.10) | copy-start | bytes 786436
  22.0 123.9 %copy-start.4 = (f32[256,256]{1,0:T(8,128)S(1)}, f32[256,256]{1,0:T(8,128)}, u32[]{:S(2)}) copy-start(f32[256,256]{1,0:T(8,128)} %param.9) | copy-start | bytes 786436
  22.0 166.7 %reduce-scatter.5.cloned.1.call-start = ((), (), s32[]{:S(2)}) async-start(), calls=%async_computation.4 | async-start | bytes 2359296 | tf_op jit(solution)/shard_map/reduce_scatter | solution.py:53
  146.9 121.3 %copy-start.1 = (f32[256,256]{1,0:T(8,128)}, f32[256,256]{1,0:T(8,128)S(1)}, u32[]{:S(2)}) copy-start(f32[256,256]{1,0:T(8,128)S(1)} %get-tuple-element.4) | copy-start | bytes 786436
  146.9 121.3 %copy-start.2 = (f32[256,256]{1,0:T(8,128)}, f32[256,256]{1,0:T(8,128)S(1)}, u32[]{:S(2)}) copy-start(f32[256,256]{1,0:T(8,128)S(1)} %get-tuple-element.5) | copy-start | bytes 786436
  148.8 107.2 %all-gather.2.cloned.1.call-start = ((), (), s32[]{:S(2)}) async-start(), calls=%async_computation.2 | async-start | bytes 4325376 | tf_op jit(solution)/shard_map/all_gather | solution.py:30
  189.6 78.6 %copy-start.5 = (f32[4,2,256,32]{2,3,1,0:T(8,128)S(1)}, f32[4,2,256,32]{2,3,1,0:T(8,128)}, u32[]{:S(2)}) copy-start(f32[4,2,256,32]{2,3,1,0:T(8,128)} %reduce-scatter.5.cloned.1.call-done) | copy-start | bytes 786436
  189.7 78.6 %collective-permute-start = (f32[4,2,128,32]{2,3,1,0:T(8,128)S(1)}, f32[4,2,128,32]{2,3,1,0:T(8,128)S(1)}, u32[]{:S(2)}, u32[]{:S(2)}) collective-permute-start(f32[4,2,128,32]{2,3,1,0:T(8,128)S(1)} %constant_dynamic-slice_fusion), channel_id=1, source_target_pairs={{0,8},{8,0},{16,24},{24,16},{32,40},{40,32},{48,56},{56,48},{64,72... | collective-permute-start | bytes 393224 | tf_op jit(solution)/shard_map/ppermute | solution.py:13
Sparse Core Ops, SparseCore 0:
  22.1 123.7 reduce-scatter.2
  148.9 39.7 reduce-scatter.4
  191.3 64.6 all-gather.1
where the time goes:
time: 276 us; the launch traced here: 275 us
  waiting for transfers between devices  223 us (81%)
  matrix products  26 us (9%)
  between operations  13.8 us (5%)
  starting transfers between devices  6.01 us (2%)
  other arithmetic  3.5 us (1%)
  local copies, waits for them, and re-layouts  2.77 us (1%)
    reduce_scatter x1, waiting for transfers between devices, local(): lax.psum_scatter(lax.dot_general(columns, kv_cotangent, contract, preferr...  123 us
    all_gather x1, waiting for transfers between devices, local(): lax.all_gather(kv_weight, 'fsdp', axis=0, tiled=True)  60.5 us
    reduce_scatter x1, waiting for transfers between devices, local(): lax.psum_scatter(contribution, 'tp', scatter_dimension=3, tiled=True)  39.2 us
    dot_general x1, matrix products, local(): lax.dot_general(columns, kv_cotangent, contract, preferred_element_type=j...  13.7 us
    dot_general x1, matrix products, local(): jnp.dot(columns, lax.all_gather(kv_weight, 'fsdp', axis=0, tiled=True), p...  12.2 us
    ppermute x1, starting transfers between devices, from_partner(): lax.ppermute(shard, axis, [(i, i ^ 1 << bit) for i in range(lax.axis_size...  5.89 us
  transfers between devices with their start and end apart: 4, of which 3 were waited for; matrix products, arithmetic and copies ran while one was open for 5% of the time, Pallas kernels for 0%

commit v1 on v0

--- a/solution.py
+++ b/solution.py
@@ -25,11 +25,14 @@
 def local(normed, kv_weight, kv_cotangent, first_moment, second_moment, cauchy_points):
     contract = (((0,), (0,)), ((), ()))
     columns = normed
-    projected = jnp.dot(
-        columns,
-        lax.all_gather(kv_weight, "fsdp", axis=0, tiled=True),
-        preferred_element_type=jnp.float32,
-    )
+
+    def raise_the_trees(inner_x):
+        r1 = lax.axis_size("fsdp")
+        long_array = jnp.stack(r1 * [inner_x], axis=0)
+        piece_out = lax.all_to_all(long_array, axis_name="fsdp", split_axis=0, concat_axis=0)
+        return jnp.concatenate(piece_out, axis=0)
+
+    projected = jnp.dot(columns, raise_the_trees(kv_weight), preferred_element_type=jnp.float32)
     keys_values = projected.astype(jnp.bfloat16)
     columns = normed
     gradient = lax.psum_scatter(

time: 276 us -> 262 us (0.949)
  waiting for transfers between devices: 223 us -> 194 us
  starting transfers between devices: 6.01 us -> 18.8 us
    all_gather x1 -> x0, waiting for transfers between devices: 60.5 us -> none  [local(): lax.all_gather(kv_weight, 'fsdp', axis=0, tiled=True)]
    reduce_scatter x1, waiting for transfers between devices: 123 us -> 154 us  [local(): lax.psum_scatter(lax.dot_general(columns, kv_cotangent, contract, preferr...]
    all_to_all x0 -> x1, starting transfers between devices: none -> 12.8 us  [raise_the_trees(): lax.all_to_all(long_array, axis_name='fsdp', split_axis=0, concat_axis=0)]
  transfers between devices with their start and end apart: 4 -> 4, of which waited for: 3 -> 2; matrix products, arithmetic and copies ran while one was open for 5% -> 7% of each run, Pallas kernels for 0% -> 0%
where the time goes in v1:
time: 262 us
  waiting for transfers between devices  194 us (74%)
  matrix products  26 us (10%)
  starting transfers between devices  18.8 us (7%)
  between operations  14.1 us (5%)
  local copies, waits for them, and re-layouts  5.48 us (2%)
  other arithmetic  3.52 us (1%)
    reduce_scatter x1, waiting for transfers between devices, local(): lax.psum_scatter(lax.dot_general(columns, kv_cotangent, contract, preferr...  154 us
    reduce_scatter x1, waiting for transfers between devices, local(): lax.psum_scatter(contribution, 'tp', scatter_dimension=3, tiled=True)  39.9 us
    dot_general x1, matrix products, local(): lax.dot_general(columns, kv_cotangent, contract, preferred_element_type=j...  13.7 us
    all_to_all x1, starting transfers between devices, raise_the_trees(): lax.all_to_all(long_array, axis_name='fsdp', split_axis=0, concat_axis=0)  12.8 us
    dot_general x1, matrix products, local(): jnp.dot(columns, raise_the_trees(kv_weight), preferred_element_type=jnp.f...  12.3 us
    ppermute x1, starting transfers between devices, from_partner(): lax.ppermute(shard, axis, [(i, i ^ 1 << bit) for i in range(lax.axis_size...  5.89 us
  transfers between devices with their start and end apart: 4, of which 2 were waited for; matrix products, arithmetic and copies ran while one was open for 7% of the time, Pallas kernels for 0%

profile of v1, /device:TPU:1, one launch (start us, length us, event | category | flops | bytes accessed | tf_op | source)
XLA Modules:
  0.0 262.1 jit_solution(5918644207596438836)
XLA Ops:
  7.2 0.0 copy-start
  7.2 0.0 reduce-scatter.3.cloned.1.call-start
  7.2 1.0 copy-done
  8.2 13.7 %fusion.1 = f32[8192,256]{1,0:T(8,128)} fusion(bf16[1024,8192]{1,0:T(8,128)(2,1)} %param.6, bf16[1024,256]{1,0:T(8,128)(2,1)S(1)} %copy-done), kind=kOutput, calls=%fused_computation.10 | convolution fusion | flops 4294967296 | bytes 25690112 | tf_op jit(solution)/shard_map/dot_general | solution.py:39
  22.0 0.0 reduce-scatter.3.cloned.1.call-update
  22.0 0.9 copy-done.6
  22.9 2.4 stack.8
  25.3 12.8 %all-to-all-start = ((bf16[32,256,256]{2,1,0:T(8,128)(2,1)}), bf16[32,256,256]{2,1,0:T(8,128)(2,1)}, u32[]{:S(2)}, u32[]{:S(2)}) async-start(bf16[32,256,256]{2,1,0:T(8,128)(2,1)} %stack.8), calls=%async_computation | async-start | bytes 8388608 | tf_op jit(solution)/shard_map/all_to_all | solution.py:32
  38.1 0.0 reduce-scatter.5.cloned.1.call-start
  38.2 0.1 slice.7
  38.2 0.2 multiply_reduce_fusion
  38.4 154.3 %reduce-scatter.3.cloned.1.call-done = f32[256,256]{1,0:T(8,128)} async-done(((f32[8192,256]{1,0:T(8,128)}), f32[256,256]{1,0:T(8,128)}) %reduce-scatter.3.cloned.1.call-update) | async-done | bytes 262160 | tf_op jit(solution)/shard_map/reduce_scatter | solution.py:38
  192.7 1.0 fusion
  193.7 0.0 copy-start.1
  193.8 0.0 copy-start.2
  193.8 0.2 copy.11
  194.0 1.6 broadcast_multiply_fusion
  195.6 0.0 reduce-scatter.5.cloned.1.call-update
  195.6 39.9 %reduce-scatter.5.cloned.1.call-done = f32[4,2,256,32]{2,3,1,0:T(8,128)} async-done(((f32[4,2,256,256]{2,3,1,0:T(8,128)}), f32[4,2,256,32]{2,3,1,0:T(8,128)}) %reduce-scatter.5.cloned.1.call-update) | async-done | bytes 262160 | tf_op jit(solution)/shard_map/reduce_scatter | solution.py:56
  235.5 0.9 constant_dynamic-slice_fusion
  236.4 5.9 %collective-permute-start = (f32[4,2,128,32]{2,3,1,0:T(8,128)S(1)}, f32[4,2,128,32]{2,3,1,0:T(8,128)S(1)}, u32[]{:S(2)}, u32[]{:S(2)}) collective-permute-start(f32[4,2,128,32]{2,3,1,0:T(8,128)S(1)} %constant_dynamic-slice_fusion), channel_id=1, source_target_pairs={{0,8},{8,0},{16,24},{24,16},{32,40},{40,32},{48,56},{56,48},{64,72... | collective-permute-start | bytes 393224 | tf_op jit(solution)/shard_map/ppermute | solution.py:13
  242.3 0.0 all-to-all-done
  242.3 12.3 %convolution_convert_fusion = bf16[1024,256]{1,0:T(8,128)(2,1)} fusion(bf16[1024,8192]{1,0:T(8,128)(2,1)} %param.6, bf16[8192,256]{1,0:T(8,128)(2,1)} %bitcast), kind=kOutput, calls=%fused_computation | convolution fusion | flops 4295229440 | bytes 21495808 | tf_op jit(solution)/shard_map/dot_general | solution.py:35
  254.6 0.7 dynamic-slice_add_fusion
  (15 shorter events, 0.1 us)
Async XLA Ops:
  7.2 1.0 copy-start
  7.2 185.5 %reduce-scatter.3.cloned.1.call-start = ((), (), s32[]{:S(2)}) async-start(), calls=%async_computation.3 | async-start | bytes 8650752 | tf_op jit(solution)/shard_map/reduce_scatter | solution.py:38
  22.0 0.9 copy-start.6
  22.9 15.3 %copy-start.7 = (s32[20]{0:T(128)S(1)}, s32[20]{0:T(128)}, u32[]{:S(2)}) copy-start(s32[20]{0:T(128)} %param.11) | copy-start | bytes 244
  22.9 169.8 %copy-start.3 = (f32[256,256]{1,0:T(8,128)S(1)}, f32[256,256]{1,0:T(8,128)}, u32[]{:S(2)}) copy-start(f32[256,256]{1,0:T(8,128)} %param.10) | copy-start | bytes 786436
  22.9 169.8 %copy-start.4 = (f32[256,256]{1,0:T(8,128)S(1)}, f32[256,256]{1,0:T(8,128)}, u32[]{:S(2)}) copy-start(f32[256,256]{1,0:T(8,128)} %param.9) | copy-start | bytes 786436
  25.3 217.0 %all-to-all-start = ((bf16[32,256,256]{2,1,0:T(8,128)(2,1)}), bf16[32,256,256]{2,1,0:T(8,128)(2,1)}, u32[]{:S(2)}, u32[]{:S(2)}) async-start(bf16[32,256,256]{2,1,0:T(8,128)(2,1)} %stack.8), calls=%async_computation | async-start | bytes 8388608 | tf_op jit(solution)/shard_map/all_to_all | solution.py:32
  38.1 197.4 %reduce-scatter.5.cloned.1.call-start = ((), (), s32[]{:S(2)}) async-start(), calls=%async_computation.4 | async-start | bytes 2359296 | tf_op jit(solution)/shard_map/reduce_scatter | solution.py:56
  193.7 60.9 %copy-start.1 = (f32[256,256]{1,0:T(8,128)}, f32[256,256]{1,0:T(8,128)S(1)}, u32[]{:S(2)}) copy-start(f32[256,256]{1,0:T(8,128)S(1)} %get-tuple-element.4) | copy-start | bytes 786436
  193.8 60.9 %copy-start.2 = (f32[256,256]{1,0:T(8,128)}, f32[256,256]{1,0:T(8,128)S(1)}, u32[]{:S(2)}) copy-start(f32[256,256]{1,0:T(8,128)S(1)} %get-tuple-element.5) | copy-start | bytes 786436
  236.4 18.2 %collective-permute-start = (f32[4,2,128,32]{2,3,1,0:T(8,128)S(1)}, f32[4,2,128,32]{2,3,1,0:T(8,128)S(1)}, u32[]{:S(2)}, u32[]{:S(2)}) collective-permute-start(f32[4,2,128,32]{2,3,1,0:T(8,128)S(1)} %constant_dynamic-slice_fusion), channel_id=1, source_target_pairs={{0,8},{8,0},{16,24},{24,16},{32,40},{40,32},{48,56},{56,48},{64,72... | collective-permute-start | bytes 393224 | tf_op jit(solution)/shard_map/ppermute | solution.py:13
  242.3 12.3 %copy-start.5 = (f32[4,2,256,32]{2,3,1,0:T(8,128)S(1)}, f32[4,2,256,32]{2,3,1,0:T(8,128)}, u32[]{:S(2)}) copy-start(f32[4,2,256,32]{2,3,1,0:T(8,128)} %reduce-scatter.5.cloned.1.call-done) | copy-start | bytes 786436
Sparse Core Ops, SparseCore 0:
  22.1 170.5 reduce-scatter.2
  195.8 39.7 reduce-scatter.4
